TPU v7x, 256 devices: a whole 4x4x8 slice. The times are simulated.
256 devices in a mesh: tm: 64 (over z, x, core), row: 4 (over y).
Axes of the slice: x: 4, y: 4, z: 8, core: 2. Of those that a mesh axis runs over, the one named last changes fastest.
Arguments:
- filter_map: bfloat16 [1024, 256, 256], P('tm', 'row'), may hold values from -1 to 1
- filter_cov: bfloat16 [1024, 256, 256], P('tm', 'row'), may hold values from -1 to 1
- smoother_gain: bfloat16 [1024, 256, 256], P('tm', 'row'), may hold values from -1 to 1
- transition: bfloat16 [256, 256], replicated, may hold values from -0.375 to 0.375
- site_basis: bfloat16 [2048, 256], replicated, may hold values from -0.375 to 0.375
- obs_time: int32 [32768], P('tm'), may hold values from 0 to 1023, as said below
- obs_site: int32 [32768], P('tm'), may hold values from 0 to 2047
- obs_value: float32 [32768, 128], P('tm'), may hold values from -6 to 6
- obs_weight: float32 [32768], P('tm'), may hold values from 0.5 to 8
Outputs:
- smoothed: float32 [1024, 256, 128], P('tm', 'row')
Inputs may be any that keep to these rules, and one draw needn't show every extreme that they name: `obs_time`: row r has a time step from (r // 512) * 16 to (r // 512 + 1) * 16 - 1; rows are in no order of time.
All inputs are finite; a program needn't handle non-finite values.
Results may differ from a plain program's by a relative error of at most 0.0041.
Values may be sent and summed in bfloat16 or wider, within the bound.
No kernel may reach another device: no remote copies, remote signals or barrier semaphores. Data moves between devices by JAX's collectives and lax.ppermute only.
A program may use at most 128 MiB of HBM per device.

v0:
```python
import jax
import jax.numpy as jnp
from jax import lax
from jax.sharding import PartitionSpec as P

highest = lax.Precision.HIGHEST


def entering(value, axis, join, neutral, backward):
    count, mine = (lax.axis_size(axis), lax.axis_index(axis))
    pieces = jax.tree.map(lambda part: lax.all_gather(part, axis), value)
    if backward:
        pieces = jax.tree.map(lambda part: part[::-1], pieces)
        mine = count - 1 - mine
    running = jax.tree.map(
        lambda part, zero: jnp.full_like(part, 0) + jnp.asarray(zero, part.dtype), value, neutral
    )

    def step(position, running):
        longer = join(running, jax.tree.map(lambda part: part[position], pieces))
        return jax.tree.map(lambda new, old: jnp.where(position < mine, new, old), longer, running)

    return lax.fori_loop(0, count - 1, step, running)


def product(first_factor, second_factor):
    return jnp.dot(
        first_factor, second_factor, precision=highest, preferred_element_type=jnp.float32
    )


def compose(earlier, later):
    return (product(later[0], earlier[0]), product(later[0], earlier[1]) + later[1])


def gain_at(gain_matrix, last_flag):
    return jnp.where(last_flag, jnp.zeros((), jnp.float32), gain_matrix.astype(jnp.float32))


def build_information(obs_time, obs_site, obs_value, obs_weight, site_basis, num_steps):
    local_time = obs_time - lax.axis_index("tm") * num_steps
    basis_rows = jnp.take(site_basis, obs_site, axis=0)
    weighted = (obs_weight[:, None] * obs_value).astype(jnp.bfloat16)

    def one_step(time_step_index):
        masked = jnp.where(
            (local_time == time_step_index)[:, None], basis_rows, jnp.zeros((), jnp.bfloat16)
        )
        summed = lax.dot_general(
            masked, weighted, (((0,), (0,)), ((), ())), preferred_element_type=jnp.float32
        )
        return summed.astype(jnp.bfloat16)

    return lax.map(one_step, jnp.arange(num_steps, dtype=jnp.int32))


def forward_prefix(summary, identity_pair):
    return entering((summary[0], summary[1]), "tm", compose, identity_pair, False)


def backward_prefix(summary, identity_pair):
    return entering((summary[0], summary[1]), "tm", compose, identity_pair, True)


def offset_terms(gains, mean_share, filtered, transition_wide, final_flags):

    def one_offset(running, inputs):
        gain_matrix, mean_part, mean_whole, last_flag = inputs
        pushed = product(transition_wide, mean_whole)
        corrected = mean_part - product(gain_at(gain_matrix, last_flag), pushed)
        return (running, jnp.where(last_flag, mean_part, corrected))

    return lax.scan(one_offset, 0, (gains, mean_share, filtered, final_flags))[1]


def whole_passes(maps_whole, gains_whole, drive_whole, transition_wide, final_flags, identity_pair):

    def summary_step(running, inputs):
        return (compose(running, (inputs[0].astype(jnp.float32), inputs[1])), None)

    summary = lax.scan(summary_step, identity_pair, (maps_whole, drive_whole))[0]
    incoming = forward_prefix(summary, identity_pair)

    def filter_step(current, inputs):
        current = product(inputs[0].astype(jnp.float32), current) + inputs[1]
        return (current, current)

    filtered = lax.scan(filter_step, incoming[1], (maps_whole, drive_whole))[1]
    offsets = offset_terms(gains_whole, filtered, filtered, transition_wide, final_flags)

    def smooth_summary(running, inputs):
        return (compose(running, (gain_at(inputs[0], inputs[2]), inputs[1])), None)

    back_summary = lax.scan(
        smooth_summary, identity_pair, (gains_whole, offsets, final_flags), reverse=True
    )[0]
    outgoing = backward_prefix(back_summary, identity_pair)

    def smooth_step(current, inputs):
        current = product(gain_at(inputs[0], inputs[2]), current) + inputs[1]
        return (current, current)

    return lax.scan(smooth_step, outgoing[1], (gains_whole, offsets, final_flags), reverse=True)[1]


def local(
    filter_map,
    filter_cov,
    smoother_gain,
    transition,
    site_basis,
    obs_time,
    obs_site,
    obs_value,
    obs_weight,
):
    num_steps = filter_map.shape[0]
    row_count = filter_map.shape[1]
    state_width = filter_map.shape[2]
    members = obs_value.shape[1]
    row_start = lax.axis_index("row") * row_count
    is_final = lax.axis_index("tm") == lax.axis_size("tm") - 1
    final_flags = jnp.logical_and(is_final, jnp.arange(num_steps) == num_steps - 1)
    identity = jnp.eye(state_width, dtype=jnp.float32)
    transition_wide = transition.astype(jnp.float32)
    identity_pair = (identity, jnp.zeros((state_width, members), jnp.float32))
    information = build_information(
        obs_time, obs_site, obs_value, obs_weight, site_basis, num_steps
    )
    maps_whole, gains_whole, covs_whole = (
        lax.all_gather(filter_map, "row", axis=1, tiled=True),
        lax.all_gather(smoother_gain, "row", axis=1, tiled=True),
        lax.all_gather(filter_cov, "row", axis=1, tiled=True),
    )
    drive_whole = jnp.einsum(
        "kij,kje->kie", covs_whole, information, preferred_element_type=jnp.float32
    )
    smoothed = whole_passes(
        maps_whole, gains_whole, drive_whole, transition_wide, final_flags, identity_pair
    )
    return lax.dynamic_slice_in_dim(smoothed, row_start, row_count, 1)


def solution(mesh):
    placed = (
        P("tm", "row", None),
        P("tm", "row", None),
        P("tm", "row", None),
        P(),
        P(),
        P("tm"),
        P("tm"),
        P("tm", None),
        P("tm"),
    )
    return jax.shard_map(
        local, mesh=mesh, in_specs=placed, out_specs=P("tm", "row", None), check_vma=False
    )
```

profile of v0, /device:TPU:1, one launch (start us, length us, event | category | flops | bytes accessed | tf_op | source)
XLA Modules:
  0.0 877.9 jit_solution(3602552848383626959)
XLA Ops:
  12.4 38.2 %while.106 = (s32[]{:T(128)}, bf16[16,256,128]{2,1,0:T(8,128)(2,1)}, s32[16]{0:T(128)S(1)}, s32[512]{0:T(512)S(1)}, bf16[512,256]{1,0:T(8,128)(2,1)S(1)}, /*index=5*/bf16[512,128]{1,0:T(8,128)(2,1)S(1)}, s32[]{:T(128)}) while((s32[]{:T(128)}, bf16[16,256,128]{2,1,0:T(8,128)(2,1)}, s32[16]{0:T(128)S(1)}, s32[512]{0:T(512)S(1)}, ...), condition=%wide.region_1.2_spmd, body=%wide.region_0.1_spmd.sunk | while | flops 33718784 | bytes 462429 | solution.py:54
  50.7 2.7 convolution_bitcast_fusion
  55.3 26.1 %all-gather.14.cloned.1.call-done = bf16[16,256,256]{2,1,0:T(8,128)(2,1)} async-done(((bf16[16,64,256]{2,1,0:T(8,128)(2,1)}), bf16[16,256,256]{2,1,0:T(8,128)(2,1)}) %all-gather.14.cloned.1.call-update) | async-done | bytes 2097168 | tf_op jit(solution)/shard_map/all_gather | solution.py:131
  81.4 40.7 %while.110 = (s32[]{:T(128)}, f32[256,256]{1,0:T(8,128)S(1)}, f32[256,128]{1,0:T(8,128)S(1)}, bf16[16,256,256]{2,1,0:T(8,128)(2,1)}, f32[16,256,128]{2,1,0:T(8,128)}, /*index=5*/s32[]{:T(128)}, s32[]{:T(128)}) while((s32[]{:T(128)}, f32[256,256]{1,0:T(8,128)S(1)}, f32[256,128]{1,0:T(8,128)S(1)}, bf16[16,256,256]{2,1,0:T(8,128)(2,1)}, ...), condition=%wide.region_3.4_spmd.clone, body=%wide.region_2.3_spmd.clone.sunk | while | flops 302055424 | bytes 1967703 | solution.py:81
  124.1 82.4 %all-gather.20.cloned.1.call-done = f32[16384,128]{1,0:T(8,128)} async-done(((f32[256,128]{1,0:T(8,128)}), f32[16384,128]{1,0:T(8,128)}) %all-gather.20.cloned.1.call-update) | async-done | bytes 8388624 | tf_op jit(solution)/shard_map/all_gather | solution.py:11
  206.5 98.7 %all-gather.18.cloned.1.call-done = f32[16384,256]{1,0:T(8,128)} async-done(((f32[256,256]{1,0:T(8,128)}), f32[16384,256]{1,0:T(8,128)}) %all-gather.18.cloned.1.call-update) | async-done | bytes 16777232 | tf_op jit(solution)/shard_map/all_gather | solution.py:11
  305.2 89.4 %while.111 = (s32[]{:T(128)}, f32[256,128]{1,0:T(8,128)S(1)}, s32[]{:T(128)}, f32[64,256,256]{2,1,0:T(8,128)}, f32[64,256,128]{2,1,0:T(8,128)}, /*index=5*/s32[]{:T(128)}, s32[]{:T(128)}) while((s32[]{:T(128)}, f32[256,128]{1,0:T(8,128)S(1)}, s32[]{:T(128)}, f32[64,256,256]{2,1,0:T(8,128)}, f32[64,256,128]{2,1,0:T(8,128)}, ...), condition=%wide.region_5.6_spmd.clone, body=%wide.region_4.5_spmd.clone.sunk | while | flops 100794368 | bytes 1051231 | solution.py:23
  394.7 20.7 %while.107 = (s32[]{:T(128)}, f32[256,128]{1,0:T(8,128)S(1)}, f32[16,256,128]{2,1,0:T(8,128)S(1)}, bf16[16,256,256]{2,1,0:T(8,128)(2,1)}, f32[16,256,128]{2,1,0:T(8,128)}, /*index=5*/s32[]{:T(128)}) while((s32[]{:T(128)}, f32[256,128]{1,0:T(8,128)S(1)}, f32[16,256,128]{2,1,0:T(8,128)S(1)}, bf16[16,256,256]{2,1,0:T(8,128)(2,1)}, ...), condition=%wide.region_7.8_spmd, body=%wide.region_6.7_spmd.sunk | while | flops 100696064 | bytes 918597 | solution.py:88
  417.0 57.1 %while.108 = (s32[]{:T(128)}, f32[16,256,128]{2,1,0:T(8,128)}, pred[16]{0:T(512)(128)(4,1)S(1)}, f32[16,256,128]{2,1,0:T(8,128)S(1)}, bf16[16,256,256]{2,1,0:T(8,128)(2,1)}, /*index=5*/f32[256,256]{1,0:T(8,128)S(1)}, s32[]{:T(128)}) while((s32[]{:T(128)}, f32[16,256,128]{2,1,0:T(8,128)}, pred[16]{0:T(512)(128)(4,1)S(1)}, ...), condition=%wide.region_9.10_spmd, body=%wide.region_8.9_spmd.sunk | while | flops 201523200 | bytes 1050711 | solution.py:73
  418.0 2.6 fusion.121
  421.6 2.6 fusion.121
  425.1 2.6 fusion.121
  428.7 2.6 fusion.121
  432.3 2.6 fusion.121
  435.9 2.6 fusion.121
  439.4 2.6 fusion.121
  443.0 2.6 fusion.121
  446.6 2.6 fusion.121
  450.2 2.6 fusion.121
  453.7 2.6 fusion.121
  457.3 2.6 fusion.121
  460.8 2.6 fusion.121
  464.4 2.6 fusion.121
  468.0 2.6 fusion.121
  471.5 2.6 fusion.121
  474.1 73.4 %while.112 = (s32[]{:T(128)}, f32[256,256]{1,0:T(8,128)S(1)}, f32[256,128]{1,0:T(8,128)S(1)}, pred[16]{0:T(512)(128)(4,1)S(1)}, bf16[16,256,256]{2,1,0:T(8,128)(...) while((s32[]{:T(128)}, f32[256,256]{1,0:T(8,128)S(1)}, ...), condition=%wide.region_11.12_spmd.clone, body=%wide.region_10.11_spmd.clone.sunk | while | flops 302317568 | bytes 1968764 | solution.py:94
  549.0 79.4 %all-gather.24.cloned.1.call-done = f32[16384,128]{1,0:T(8,128)} async-done(((f32[256,128]{1,0:T(8,128)}), f32[16384,128]{1,0:T(8,128)}) %all-gather.24.cloned.1.call-update) | async-done | bytes 8388624 | tf_op jit(solution)/shard_map/all_gather | solution.py:11
  628.3 7.6 rev.7
  636.0 91.2 %all-gather.22.cloned.1.call-done = f32[16384,256]{1,0:T(8,128)} async-done(((f32[256,256]{1,0:T(8,128)}), f32[16384,256]{1,0:T(8,128)}) %all-gather.22.cloned.1.call-update) | async-done | bytes 16777232 | tf_op jit(solution)/shard_map/all_gather | solution.py:11
  727.2 11.5 %rev.6 = f32[64,256,256]{2,1,0:T(8,128)} reverse(f32[64,256,256]{2,1,0:T(8,128)} %bitcast.136), dimensions={0} | reverse | bytes 33554432 | tf_op jit(solution)/shard_map/rev | solution.py:13
  738.7 89.4 %while.113 = (s32[]{:T(128)}, f32[256,128]{1,0:T(8,128)S(1)}, s32[]{:T(128)}, f32[64,256,256]{2,1,0:T(8,128)}, f32[64,256,128]{2,1,0:T(8,128)}, /*index=5*/s32[]{:T(128)}, s32[]{:T(128)}) while((s32[]{:T(128)}, f32[256,128]{1,0:T(8,128)S(1)}, s32[]{:T(128)}, f32[64,256,256]{2,1,0:T(8,128)}, f32[64,256,128]{2,1,0:T(8,128)}, ...), condition=%wide.region_13.14_spmd.clone, body=%wide.region_12.13_spmd.clone.sunk | while | flops 100794368 | bytes 1051231 | solution.py:23
  828.3 41.9 %while.109 = (s32[]{:T(128)}, f32[256,128]{1,0:T(8,128)S(1)}, f32[16,256,128]{2,1,0:T(8,128)S(1)}, pred[16]{0:T(512)(128)(4,1)S(1)}, bf16[16,256,256]{2,1,0:T(8,...) while((s32[]{:T(128)}, f32[256,128]{1,0:T(8,128)S(1)}, f32[16,256,128]{2,1,0:T(8,128)S(1)}, ...), condition=%wide.region_15.16_spmd, body=%wide.region_14.15_spmd.sunk | while | flops 100827136 | bytes 919143 | solution.py:103
  (612 shorter events, 416.1 us)
Async XLA Ops:
  6.5 3.6 copy-start
  6.5 5.7 copy-start.6
  6.5 5.7 copy-start.8
  6.5 44.1 %all-gather.16.cloned.1.call-start = ((), (), s32[]{:S(2)}) async-start(), calls=%async_computation.2 | async-start | bytes 2621440 | tf_op jit(solution)/shard_map/all_gather | solution.py:133
  7.3 74.1 %all-gather.14.cloned.1.call-start = ((), (), s32[]{:S(2)}) async-start(), calls=%async_computation.1 | async-start | bytes 2621440 | tf_op jit(solution)/shard_map/all_gather | solution.py:131
  8.0 198.5 %all-gather.20.cloned.1.call-start = ((), (), s32[]{:S(2)}) async-start(), calls=%async_computation.4 | async-start | bytes 8519680 | tf_op jit(solution)/shard_map/all_gather | solution.py:11
  81.4 42.6 %copy-start.7 = (bf16[256,256]{1,0:T(8,128)(2,1)S(1)}, bf16[256,256]{1,0:T(8,128)(2,1)}, u32[]{:S(2)}) copy-start(bf16[256,256]{1,0:T(8,128)(2,1)} %param.28) | copy-start | bytes 393220
  122.1 0.7 copy-start.5
  122.1 0.7 copy-start.3
  122.8 182.4 %all-gather.18.cloned.1.call-start = ((), (), s32[]{:S(2)}) async-start(), calls=%async_computation.3 | async-start | bytes 17039360 | tf_op jit(solution)/shard_map/all_gather | solution.py:11
  123.4 292.1 %all-gather.12.cloned.1.call-start = ((), (), s32[]{:S(2)}) async-start(), calls=%async_computation | async-start | bytes 2621440 | tf_op jit(solution)/shard_map/all_gather | solution.py:132
  123.9 504.4 %all-gather.24.cloned.1.call-start = ((), (), s32[]{:S(2)}) async-start(), calls=%async_computation.6 | async-start | bytes 8519680 | tf_op jit(solution)/shard_map/all_gather | solution.py:11
  547.5 0.7 copy-start.4
  547.6 0.7 copy-start.2
  548.2 178.9 %all-gather.22.cloned.1.call-start = ((), (), s32[]{:S(2)}) async-start(), calls=%async_computation.5 | async-start | bytes 17039360 | tf_op jit(solution)/shard_map/all_gather | solution.py:11
  828.3 42.8 %copy-start.1 = (bf16[2048,256]{1,0:T(8,128)(2,1)S(1)}, bf16[2048,256]{1,0:T(8,128)(2,1)}, u32[]{:S(2)}) copy-start(bf16[2048,256]{1,0:T(8,128)(2,1)} %param.29) | copy-start | bytes 3145732
Sparse Core Ops, SparseCore 0:
  9.1 36.9 all-gather.15
  48.0 33.3 all-gather.13
  122.9 83.5 all-gather.19
  209.1 96.0 all-gather.17
  306.8 29.7 all-gather.11
  548.3 79.9 all-gather.23
  631.1 96.0 all-gather.21
where the time goes:
time: 883 us; the launch traced here: 878 us
  matrix products  394 us (45%)
  waiting for transfers between devices  381 us (43%)
  local copies, waits for them, and re-layouts  68.6 us (8%)
  between operations  13.8 us (2%)
  other arithmetic  13.5 us (2%)
    dot_general x254, matrix products, product(): jnp.dot(first_factor, second_factor, precision=highest, preferred_element...  375 us
    all_gather x4, waiting for transfers between devices, entering(): pieces = jax.tree.map(lambda part: lax.all_gather(part, axis), value)  352 us
    dynamic_slice x48, local copies, waits for them, and re-layouts, offset_terms(): lax.scan(one_offset, 0, (gains, mean_share, filtered, final_flags))[1]  28.3 us
    all_gather x1, waiting for transfers between devices, local(): lax.all_gather(filter_map, 'row', axis=1, tiled=True)  26.1 us
    rev x2, local copies, waits for them, and re-layouts, entering(): pieces = jax.tree.map(lambda part: part[::-1], pieces)  19.1 us
  transfers between devices with their start and end apart: 7, of which 5 were waited for; matrix products, arithmetic and copies ran while one was open for 18% of the time, Pallas kernels for 0%

commit v1 on v0

--- a/solution.py
+++ b/solution.py
@@ -2,8 +2,14 @@
 import jax.numpy as jnp
 from jax import lax
 from jax.sharding import PartitionSpec as P
+from jax.lax import all_to_all, psum
 
 highest = lax.Precision.HIGHEST
+
+
+def work_views_here(obj):
+    tall = jnp.stack([obj for _ in range(psum(1, "row"))], 0)
+    return jnp.concatenate(all_to_all(tall, "row", 0, 0), 1)
 
 
 def entering(value, axis, join, neutral, backward):
@@ -128,7 +134,7 @@
         obs_time, obs_site, obs_value, obs_weight, site_basis, num_steps
     )
     maps_whole, gains_whole, covs_whole = (
-        lax.all_gather(filter_map, "row", axis=1, tiled=True),
+        work_views_here(filter_map),
         lax.all_gather(smoother_gain, "row", axis=1, tiled=True),
         lax.all_gather(filter_cov, "row", axis=1, tiled=True),
     )

time: 883 us -> 868 us (0.983)
  waiting for transfers between devices: 381 us -> 358 us
    all_gather x1 -> x0, waiting for transfers between devices: 26.1 us -> none  [local(): lax.all_gather(filter_map, 'row', axis=1, tiled=True)]
  transfers between devices with their start and end apart: 7 -> 7, of which waited for: 5 -> 5; matrix products, arithmetic and copies ran while one was open for 18% -> 19% of each run, Pallas kernels for 0% -> 0%
where the time goes in v1:
time: 868 us; the launch traced here: 863 us
  matrix products  394 us (45%)
  waiting for transfers between devices  358 us (41%)
  local copies, waits for them, and re-layouts  72.7 us (8%)
  between operations  13.8 us (2%)
  other arithmetic  12.4 us (1%)
    dot_general x254, matrix products, product(): jnp.dot(first_factor, second_factor, precision=highest, preferred_element...  375 us
    all_gather x4, waiting for transfers between devices, entering(): pieces = jax.tree.map(lambda part: lax.all_gather(part, axis), value)  354 us
    dynamic_slice x48, local copies, waits for them, and re-layouts, offset_terms(): lax.scan(one_offset, 0, (gains, mean_share, filtered, final_flags))[1]  28.3 us
    rev x2, local copies, waits for them, and re-layouts, entering(): pieces = jax.tree.map(lambda part: part[::-1], pieces)  19.1 us
  transfers between devices with their start and end apart: 7, of which 5 were waited for; matrix products, arithmetic and copies ran while one was open for 19% of the time, Pallas kernels for 0%

profile of v1, /device:TPU:1, one launch (start us, length us, event | category | flops | bytes accessed | tf_op | source)
XLA Modules:
  0.0 862.5 jit_solution(12235916507256894046)
XLA Ops:
  7.3 2.6 stack.2
  9.9 5.1 all-to-all-start
  18.3 38.1 %while.106 = (s32[]{:T(128)}, bf16[16,256,128]{2,1,0:T(8,128)(2,1)}, s32[16]{0:T(128)S(1)}, s32[512]{0:T(512)S(1)}, bf16[512,256]{1,0:T(8,128)(2,1)S(1)}, /*index=5*/bf16[512,128]{1,0:T(8,128)(2,1)S(1)}, s32[]{:T(128)}) while((s32[]{:T(128)}, bf16[16,256,128]{2,1,0:T(8,128)(2,1)}, s32[16]{0:T(128)S(1)}, s32[512]{0:T(512)S(1)}, ...), condition=%wide.region_1.2_spmd, body=%wide.region_0.1_spmd.sunk | while | flops 33718784 | bytes 462429 | solution.py:60
  58.7 2.7 convolution_bitcast_fusion
  63.3 40.7 %while.110 = (s32[]{:T(128)}, f32[256,256]{1,0:T(8,128)S(1)}, f32[256,128]{1,0:T(8,128)S(1)}, bf16[16,256,256]{2,1,0:T(8,128)(2,1)}, f32[16,256,128]{2,1,0:T(8,128)}, /*index=5*/s32[]{:T(128)}, s32[]{:T(128)}) while((s32[]{:T(128)}, f32[256,256]{1,0:T(8,128)S(1)}, f32[256,128]{1,0:T(8,128)S(1)}, bf16[16,256,256]{2,1,0:T(8,128)(2,1)}, ...), condition=%wide.region_3.4_spmd.clone, body=%wide.region_2.3_spmd.clone.sunk | while | flops 302055424 | bytes 1967703 | solution.py:87
  106.1 85.0 %all-gather.17.cloned.1.call-done = f32[16384,128]{1,0:T(8,128)} async-done(((f32[256,128]{1,0:T(8,128)}), f32[16384,128]{1,0:T(8,128)}) %all-gather.17.cloned.1.call-update) | async-done | bytes 8388624 | tf_op jit(solution)/shard_map/all_gather | solution.py:17
  191.1 98.8 %all-gather.15.cloned.1.call-done = f32[16384,256]{1,0:T(8,128)} async-done(((f32[256,256]{1,0:T(8,128)}), f32[16384,256]{1,0:T(8,128)}) %all-gather.15.cloned.1.call-update) | async-done | bytes 16777232 | tf_op jit(solution)/shard_map/all_gather | solution.py:17
  289.9 89.4 %while.111 = (s32[]{:T(128)}, f32[256,128]{1,0:T(8,128)S(1)}, s32[]{:T(128)}, f32[64,256,256]{2,1,0:T(8,128)}, f32[64,256,128]{2,1,0:T(8,128)}, /*index=5*/s32[]{:T(128)}, s32[]{:T(128)}) while((s32[]{:T(128)}, f32[256,128]{1,0:T(8,128)S(1)}, s32[]{:T(128)}, f32[64,256,256]{2,1,0:T(8,128)}, f32[64,256,128]{2,1,0:T(8,128)}, ...), condition=%wide.region_5.6_spmd.clone, body=%wide.region_4.5_spmd.clone.sunk | while | flops 100794368 | bytes 1051231 | solution.py:29
  379.5 20.7 %while.107 = (s32[]{:T(128)}, f32[256,128]{1,0:T(8,128)S(1)}, f32[16,256,128]{2,1,0:T(8,128)S(1)}, bf16[16,256,256]{2,1,0:T(8,128)(2,1)}, f32[16,256,128]{2,1,0:T(8,128)}, /*index=5*/s32[]{:T(128)}) while((s32[]{:T(128)}, f32[256,128]{1,0:T(8,128)S(1)}, f32[16,256,128]{2,1,0:T(8,128)S(1)}, bf16[16,256,256]{2,1,0:T(8,128)(2,1)}, ...), condition=%wide.region_7.8_spmd, body=%wide.region_6.7_spmd.sunk | while | flops 100696064 | bytes 918597 | solution.py:94
  401.8 57.1 %while.108 = (s32[]{:T(128)}, f32[16,256,128]{2,1,0:T(8,128)}, pred[16]{0:T(512)(128)(4,1)S(1)}, f32[16,256,128]{2,1,0:T(8,128)S(1)}, bf16[16,256,256]{2,1,0:T(8,128)(2,1)}, /*index=5*/f32[256,256]{1,0:T(8,128)S(1)}, s32[]{:T(128)}) while((s32[]{:T(128)}, f32[16,256,128]{2,1,0:T(8,128)}, pred[16]{0:T(512)(128)(4,1)S(1)}, ...), condition=%wide.region_9.10_spmd, body=%wide.region_8.9_spmd.sunk | while | flops 201523200 | bytes 1050711 | solution.py:79
  402.8 2.6 fusion.121
  406.3 2.6 fusion.121
  409.9 2.6 fusion.121
  413.5 2.6 fusion.121
  417.1 2.6 fusion.121
  420.6 2.6 fusion.121
  424.2 2.6 fusion.121
  427.8 2.6 fusion.121
  431.4 2.6 fusion.121
  438.5 2.6 fusion.121
  442.1 2.6 fusion.121
  445.6 2.6 fusion.121
  449.2 2.6 fusion.121
  452.8 2.6 fusion.121
  456.3 2.6 fusion.121
  458.9 73.4 %while.112 = (s32[]{:T(128)}, f32[256,256]{1,0:T(8,128)S(1)}, f32[256,128]{1,0:T(8,128)S(1)}, pred[16]{0:T(512)(128)(4,1)S(1)}, bf16[16,256,256]{2,1,0:T(8,128)(...) while((s32[]{:T(128)}, f32[256,256]{1,0:T(8,128)S(1)}, ...), condition=%wide.region_11.12_spmd.clone, body=%wide.region_10.11_spmd.clone.sunk | while | flops 302317568 | bytes 1968764 | solution.py:100
  533.6 79.5 %all-gather.21.cloned.1.call-done = f32[16384,128]{1,0:T(8,128)} async-done(((f32[256,128]{1,0:T(8,128)}), f32[16384,128]{1,0:T(8,128)}) %all-gather.21.cloned.1.call-update) | async-done | bytes 8388624 | tf_op jit(solution)/shard_map/all_gather | solution.py:17
  613.1 7.6 rev.7
  620.8 91.1 %all-gather.19.cloned.1.call-done = f32[16384,256]{1,0:T(8,128)} async-done(((f32[256,256]{1,0:T(8,128)}), f32[16384,256]{1,0:T(8,128)}) %all-gather.19.cloned.1.call-update) | async-done | bytes 16777232 | tf_op jit(solution)/shard_map/all_gather | solution.py:17
  711.8 11.5 %rev.6 = f32[64,256,256]{2,1,0:T(8,128)} reverse(f32[64,256,256]{2,1,0:T(8,128)} %bitcast.139), dimensions={0} | reverse | bytes 33554432 | tf_op jit(solution)/shard_map/rev | solution.py:19
  723.3 89.4 %while.113 = (s32[]{:T(128)}, f32[256,128]{1,0:T(8,128)S(1)}, s32[]{:T(128)}, f32[64,256,256]{2,1,0:T(8,128)}, f32[64,256,128]{2,1,0:T(8,128)}, /*index=5*/s32[]{:T(128)}, s32[]{:T(128)}) while((s32[]{:T(128)}, f32[256,128]{1,0:T(8,128)S(1)}, s32[]{:T(128)}, f32[64,256,256]{2,1,0:T(8,128)}, f32[64,256,128]{2,1,0:T(8,128)}, ...), condition=%wide.region_13.14_spmd.clone, body=%wide.region_12.13_spmd.clone.sunk | while | flops 100794368 | bytes 1051231 | solution.py:29
  812.9 41.9 %while.109 = (s32[]{:T(128)}, f32[256,128]{1,0:T(8,128)S(1)}, f32[16,256,128]{2,1,0:T(8,128)S(1)}, pred[16]{0:T(512)(128)(4,1)S(1)}, bf16[16,256,256]{2,1,0:T(8,...) while((s32[]{:T(128)}, f32[256,128]{1,0:T(8,128)S(1)}, f32[16,256,128]{2,1,0:T(8,128)S(1)}, ...), condition=%wide.region_15.16_spmd, body=%wide.region_14.15_spmd.sunk | while | flops 100827136 | bytes 919143 | solution.py:109
  (615 shorter events, 418.9 us)
Async XLA Ops:
  6.5 8.6 copy-start
  6.5 52.2 %all-gather.13.cloned.1.call-start = ((), (), s32[]{:S(2)}) async-start(), calls=%async_computation.2 | async-start | bytes 2621440 | tf_op jit(solution)/shard_map/all_gather | solution.py:139
  9.9 5.1 copy-start.7
  9.9 5.2 copy-start.9
  9.9 46.6 %all-to-all-start = ((bf16[4,16,64,256]{3,2,1,0:T(8,128)(2,1)}), bf16[4,16,64,256]{3,2,1,0:T(8,128)(2,1)S(1)}, u32[]{:S(2)}, u32[]{:S(2)}) async-start(bf16[4,16,64,256]{3,2,1,0:T(8,128)(2,1)} %stack.2), calls=%async_computation | async-start | bytes 4194304 | tf_op jit(solution)/shard_map/all_to_all | solution.py:12
  15.0 2.2 copy-start.8
  15.0 176.1 %all-gather.17.cloned.1.call-start = ((), (), s32[]{:S(2)}) async-start(), calls=%async_computation.4 | async-start | bytes 8519680 | tf_op jit(solution)/shard_map/all_gather | solution.py:17
  63.3 42.8 %copy-start.6 = (bf16[256,256]{1,0:T(8,128)(2,1)S(1)}, bf16[256,256]{1,0:T(8,128)(2,1)}, u32[]{:S(2)}) copy-start(bf16[256,256]{1,0:T(8,128)(2,1)} %param.28) | copy-start | bytes 393220
  104.0 0.7 copy-start.5
  104.0 0.7 copy-start.3
  104.7 185.2 %all-gather.15.cloned.1.call-start = ((), (), s32[]{:S(2)}) async-start(), calls=%async_computation.3 | async-start | bytes 17039360 | tf_op jit(solution)/shard_map/all_gather | solution.py:17
  105.4 294.8 %all-gather.11.cloned.1.call-start = ((), (), s32[]{:S(2)}) async-start(), calls=%async_computation.1 | async-start | bytes 2621440 | tf_op jit(solution)/shard_map/all_gather | solution.py:138
  106.0 507.1 %all-gather.21.cloned.1.call-start = ((), (), s32[]{:S(2)}) async-start(), calls=%async_computation.6 | async-start | bytes 8519680 | tf_op jit(solution)/shard_map/all_gather | solution.py:17
  532.3 0.7 copy-start.4
  532.3 0.7 copy-start.2
  533.0 178.8 %all-gather.19.cloned.1.call-start = ((), (), s32[]{:S(2)}) async-start(), calls=%async_computation.5 | async-start | bytes 17039360 | tf_op jit(solution)/shard_map/all_gather | solution.py:17
  812.9 42.8 %copy-start.1 = (bf16[2048,256]{1,0:T(8,128)(2,1)S(1)}, bf16[2048,256]{1,0:T(8,128)(2,1)}, u32[]{:S(2)}) copy-start(bf16[2048,256]{1,0:T(8,128)(2,1)} %param.29) | copy-start | bytes 3145732
Sparse Core Ops, SparseCore 0:
  9.1 49.5 all-gather.12
  104.8 86.2 all-gather.16
  193.9 96.0 all-gather.14
  291.6 29.7 all-gather.10
  533.1 79.9 all-gather.20
  615.7 96.0 all-gather.18
